TPU v7x, 32 devices: a whole 2x2x4 slice. The times are simulated.
32 devices in a mesh: dp: 8 (over z, core), space: 4 (over y, x).
Axes of the slice: x: 2, y: 2, z: 4, core: 2. Of those that a mesh axis runs over, the one named last changes fastest.
Arguments:
- inputs: bfloat16 [8, 24, 32, 32, 256], P('dp', 'space'), may hold values from -6 to 6
- kernels: bfloat16 [2, 3, 3, 256, 256], P(None, None, None, 'dp'), may hold values from -0.125 to 0.125
- cotangent: bfloat16 [8, 24, 32, 32, 256], P('dp', 'space'), may hold values from -0.01171875 to 0.01171875
- adjacency: int32 [24, 4, 3], P('space'), may hold values from 0 to 23, as said below
Outputs:
- final_state: bfloat16 [8, 24, 32, 32, 256], P('dp', 'space')
- kernel_grads: float32 [2, 3, 3, 256, 256], P(None, None, None, 'dp')
Inputs may be any that keep to these rules, and one draw needn't show every extreme that they name: Entry [t, e] = (n, f, r): edge e of tile t meets edge f of tile n, and r = 1 where the two edges are read in opposite directions along the shared line. The relation is symmetric: adjacency[n, f] = (t, e, r). The tiles form 2 x 2 blocks on the six faces of a cube, numbered in an order drawn from the seed.
All inputs are finite; a program needn't handle non-finite values.
Results may differ from a plain program's by a relative error of at most 0.005.
Values may be sent and summed in bfloat16 or wider, within the bound.
A program may use at most 192 MiB of HBM per device.

v0:
```python
import jax
import jax.numpy as jnp
from jax import lax
from jax.sharding import PartitionSpec as P

LAYERS = 2


def edge_strips(tile_field):
    return jnp.stack(
        [
            tile_field[:, :, 0],
            tile_field[:, :, -1],
            tile_field[:, :, :, 0],
            tile_field[:, :, :, -1],
        ],
        axis=2,
    )


def orient(strips, adjacency):
    selected = strips[:, adjacency[:, :, 0], adjacency[:, :, 1]]
    flipped = (adjacency[:, :, 2] == 1)[None, :, :, None, None]
    return jnp.where(flipped, selected[:, :, :, ::-1], selected)


def neighbor_rims(tile_field, adjacency):
    gathered = lax.all_gather(edge_strips(tile_field), "space", axis=1, tiled=True)
    return orient(gathered, adjacency)


def returned_rims(rim_values, adjacency):
    gathered = lax.all_gather(rim_values, "space", axis=1, tiled=True)
    return orient(gathered, adjacency)


def with_rim(tile_field, rim_rows):
    middle = jnp.concatenate(
        [rim_rows[:, :, 2][:, :, :, None], tile_field, rim_rows[:, :, 3][:, :, :, None]], axis=3
    )
    corner = jnp.zeros(tile_field.shape[:2] + (1, tile_field.shape[4]), tile_field.dtype)
    top_row = jnp.concatenate([corner, rim_rows[:, :, 0], corner], axis=2)[:, :, None]
    bottom_row = jnp.concatenate([corner, rim_rows[:, :, 1], corner], axis=2)[:, :, None]
    return jnp.concatenate([top_row, middle, bottom_row], axis=2)


def convolve(padded, kernel):
    extent = padded.shape[2] - 2
    channels = padded.shape[-1]
    summed = jnp.zeros(padded.shape[:2] + (extent, extent, kernel.shape[-1]), jnp.float32)
    for row_off in range(3):
        for col_off in range(3):
            patches = padded[:, :, row_off : row_off + extent, col_off : col_off + extent].reshape(
                -1, channels
            )
            summed = summed + jnp.dot(
                patches, kernel[row_off, col_off], preferred_element_type=jnp.float32
            ).reshape(summed.shape)
    return summed


def weight_grad(padded, flat_grad):
    extent = padded.shape[2] - 2
    channels = padded.shape[-1]
    rows_out = []
    for row_off in range(3):
        row_list = []
        for col_off in range(3):
            patches = padded[:, :, row_off : row_off + extent, col_off : col_off + extent].reshape(
                -1, channels
            )
            row_list.append(
                lax.dot_general(
                    patches, flat_grad, (((0,), (0,)), ((), ())), preferred_element_type=jnp.float32
                )
            )
        rows_out.append(jnp.stack(row_list))
    return jnp.stack(rows_out)


def input_grad(flat_grad, kernel, padded_shape):
    extent = padded_shape[2] - 2
    full = extent + 2
    channels = padded_shape[4]
    grid_grad = flat_grad.reshape(padded_shape[:2] + (extent, extent, flat_grad.shape[-1]))
    widened = jnp.pad(grid_grad, ((0, 0), (0, 0), (2, 2), (2, 2), (0, 0)))
    pad_grad = jnp.zeros(padded_shape, jnp.float32)
    for row_off in range(3):
        for col_off in range(3):
            window = widened[
                :, :, 2 - row_off : 2 - row_off + full, 2 - col_off : 2 - col_off + full
            ].reshape(-1, flat_grad.shape[-1])
            contrib = lax.dot_general(
                window,
                kernel[row_off, col_off],
                (((1,), (1,)), ((), ())),
                preferred_element_type=jnp.float32,
            )
            pad_grad = pad_grad + contrib.reshape(padded_shape[:4] + (channels,))
    return pad_grad


def rim_strips(pad_grad):
    return jnp.stack(
        [
            pad_grad[:, :, 0, 1:-1],
            pad_grad[:, :, -1, 1:-1],
            pad_grad[:, :, 1:-1, 0],
            pad_grad[:, :, 1:-1, -1],
        ],
        axis=2,
    )


def add_rim(interior, returned):
    interior = jnp.concatenate(
        [
            interior[:, :, :1] + returned[:, :, 0][:, :, None],
            interior[:, :, 1:-1],
            interior[:, :, -1:] + returned[:, :, 1][:, :, None],
        ],
        axis=2,
    )
    interior = jnp.concatenate(
        [
            interior[:, :, :, :1] + returned[:, :, 2][:, :, :, None],
            interior[:, :, :, 1:-1],
            interior[:, :, :, -1:] + returned[:, :, 3][:, :, :, None],
        ],
        axis=3,
    )
    return interior


def reduce_grad(partial_value):
    space_total = lax.psum(partial_value, "space")
    return lax.psum_scatter(space_total, "dp", scatter_dimension=2, tiled=True)


def per_device(inputs, kernels, cotangent, adjacency):
    weights = lax.all_gather(kernels, "dp", axis=3, tiled=True)
    current = inputs
    stored = []
    for layer_num in range(LAYERS):
        padded = with_rim(current, neighbor_rims(current, adjacency))
        preact = convolve(padded, weights[layer_num])
        current = (current.astype(jnp.float32) + jax.nn.silu(preact)).astype(jnp.bfloat16)
        stored.append((padded, preact))
    upstream = cotangent.astype(jnp.float32)
    kernel_grads = [None] * LAYERS
    for layer_num in range(LAYERS - 1, -1, -1):
        padded, preact = stored[layer_num]
        logistic = jax.nn.sigmoid(preact)
        pre_grad = (upstream * logistic * (1.0 + preact * (1.0 - logistic))).astype(jnp.bfloat16)
        flat_grad = pre_grad.reshape(-1, pre_grad.shape[-1])
        kernel_grads[layer_num] = reduce_grad(weight_grad(padded, flat_grad))
        if layer_num > 0:
            pad_grad = input_grad(flat_grad, weights[layer_num], padded.shape)
            rim_values = rim_strips(pad_grad).astype(jnp.bfloat16)
            returned = returned_rims(rim_values, adjacency).astype(jnp.float32)
            upstream = add_rim(upstream + pad_grad[:, :, 1:-1, 1:-1], returned)
    return (current, jnp.stack(kernel_grads))


def solution(mesh):
    in_specs = (
        P("dp", "space", None, None, None),
        P(None, None, None, "dp", None),
        P("dp", "space", None, None, None),
        P("space", None, None),
    )
    out_specs = (P("dp", "space", None, None, None), P(None, None, None, "dp", None))
    return jax.shard_map(
        per_device, mesh=mesh, in_specs=in_specs, out_specs=out_specs, check_vma=False
    )
```

profile of v0, /device:TPU:0, one launch (start us, length us, event | category | flops | bytes accessed | tf_op | source)
XLA Modules:
  0.0 505.8 jit_solution(17748328288666397905)
XLA Ops:
  12.9 32.7 %all-gather.5.cloned.1.call-done = bf16[1,24,4,32,256]{4,3,1,2,0:T(8,128)(2,1)} async-done(((bf16[1,6,4,32,256]{4,3,1,2,0:T(8,128)(2,1)}), bf16[1,24,4,32,256]{4,3,1,2,0:T(8,128)(2,1)}) %all-gather.5.cloned.1.call-update) | async-done | bytes 1572880 | tf_op jit(solution)/shard_map/all_gather | solution.py:28
  51.8 5.4 %fusion.38 = (bf16[6,32,32,256]{3,2,1,0:T(8,128)(2,1)}, bf16[6,32,32,256]{3,2,1,0:T(8,128)(2,1)}) fusion(bf16[1,6,32,32,256]{4,3,2,1,0:T(8,128)(2,1)S(1)} %copy-done.4, bf16[1,6,32,1,256]{4,3,2,1,0:T(2,128)(2,1)S(1)} %copy.109, bf16[1,6,32,1,256]{4,3,2,1,0:T(2,128)(2,1)S(1)} %copy.110), kind=kLoop, calls=%fused_computation.68 | loop fusion | flops 12582912 | bytes 9633792 | tf_op jit(solution)/shard_map/dot_general | solution.py:56
  57.2 4.9 maximum_maximum_fusion.1
  65.4 10.3 %slice_bitcast_fusion.9 = (bf16[6,32,32,256]{3,2,1,0:T(8,128)(2,1)}, bf16[6,32,32,256]{3,2,1,0:T(8,128)(2,1)}, bf16[6,32,32,256]{3,2,1,0:T(8,128)(2,1)}, bf16[6,...) fusion(bf16[1,6,33,34,256]{4,3,2,1,0:T(8,128)(2,1)S(1)} %get-tuple-element.31, ...), kind=kLoop, calls=%fused_computation.64 | loop fusion | bytes 37748736 | tf_op jit(solution)/shard_map/dot_general | solution.py:56
  81.7 6.2 %fusion.60 = f32[6,32,32,256]{3,1,0,2:T(8,128)} fusion(bf16[6,32,32,256]{3,2,1,0:T(8,128)(2,1)S(1)} %copy-done.18, bf16[3,3,256,256]{3,2,1,0:T(8,128)(2,1)S(1)} %get-tuple-element.46), kind=kOutput, calls=%fused_computation.93 | convolution fusion | flops 805306368 | bytes 9568256 | tf_op jit(solution)/shard_map/dot_general | solution.py:56
  88.0 6.2 %fusion.62 = f32[6,32,32,256]{3,1,0,2:T(8,128)} fusion(bf16[6,32,32,256]{3,2,1,0:T(8,128)(2,1)S(1)} %copy-done.17, bf16[3,3,256,256]{3,2,1,0:T(8,128)(2,1)S(1)} %get-tuple-element.46), kind=kOutput, calls=%fused_computation.95 | convolution fusion | flops 805306368 | bytes 9568256 | tf_op jit(solution)/shard_map/dot_general | solution.py:56
  94.2 6.3 %fusion.64 = f32[6,32,32,256]{3,1,0,2:T(8,128)} fusion(bf16[6,32,32,256]{3,2,1,0:T(8,128)(2,1)S(1)} %copy-done.16, bf16[3,3,256,256]{3,2,1,0:T(8,128)(2,1)S(1)} %get-tuple-element.46), kind=kOutput, calls=%fused_computation.97 | convolution fusion | flops 805306368 | bytes 9568256 | tf_op jit(solution)/shard_map/dot_general | solution.py:56
  100.5 6.4 %fusion.66 = f32[6,32,32,256]{3,1,0,2:T(8,128)} fusion(bf16[6,32,32,256]{3,2,1,0:T(8,128)(2,1)S(1)} %copy-done.21, bf16[3,3,256,256]{3,2,1,0:T(8,128)(2,1)S(1)} %get-tuple-element.46), kind=kOutput, calls=%fused_computation.99 | convolution fusion | flops 805306368 | bytes 9568256 | tf_op jit(solution)/shard_map/dot_general | solution.py:56
  106.9 6.3 %fusion.68 = f32[6,32,32,256]{3,1,0,2:T(8,128)} fusion(bf16[6,32,32,256]{3,2,1,0:T(8,128)(2,1)S(1)} %bitcast.431, bf16[3,3,256,256]{3,2,1,0:T(8,128)(2,1)S(1)} %get-tuple-element.46), kind=kOutput, calls=%fused_computation.101 | convolution fusion | flops 805306368 | bytes 9568256 | tf_op jit(solution)/shard_map/dot_general | solution.py:56
  113.1 6.2 %fusion.70 = f32[6,32,32,256]{3,1,0,2:T(8,128)} fusion(bf16[6,32,32,256]{3,2,1,0:T(8,128)(2,1)S(1)} %copy-done.19, bf16[3,3,256,256]{3,2,1,0:T(8,128)(2,1)S(1)} %get-tuple-element.46), kind=kOutput, calls=%fused_computation.103 | convolution fusion | flops 805306368 | bytes 9568256 | tf_op jit(solution)/shard_map/dot_general | solution.py:56
  119.4 6.7 %fusion.72 = f32[6,32,32,256]{3,1,0,2:T(8,128)} fusion(bf16[6,32,32,256]{3,2,1,0:T(8,128)(2,1)S(1)} %copy-done.15, bf16[3,3,256,256]{3,2,1,0:T(8,128)(2,1)S(1)} %get-tuple-element.46), kind=kOutput, calls=%fused_computation.105 | convolution fusion | flops 805306368 | bytes 9568256 | tf_op jit(solution)/shard_map/dot_general | solution.py:56
  126.1 6.2 %fusion.74 = f32[6,32,32,256]{3,1,0,2:T(8,128)} fusion(bf16[6,32,32,256]{3,2,1,0:T(8,128)(2,1)S(1)} %copy-done.14, bf16[3,3,256,256]{3,2,1,0:T(8,128)(2,1)S(1)} %get-tuple-element.46), kind=kOutput, calls=%fused_computation.107 | convolution fusion | flops 805306368 | bytes 9568256 | tf_op jit(solution)/shard_map/dot_general | solution.py:56
  132.3 22.0 %fusion.5 = (bf16[1,6,32,32,256]{4,2,1,3,0:T(8,128)(2,1)S(1)}, f32[6,32,32,256]{3,1,0,2:T(8,128)}) fusion(bf16[1,6,32,32,256]{4,3,2,1,0:T(8,128)(2,1)S(1)} %copy-done.5, f32[6,32,32,256]{3,1,0,2:T(8,128)} %fusion.60, f32[6,32,32,256]{3,1,0,2:T(8,128)} %fusion.62, f32[6,32,32,256]{3,1,0,2:T(8,128)} %fusion.64, f32[6,32,32,256]{3,1,0,2:T(8,128)} %fusion.66, ...), kind=kOutput, calls=%fused_computation.15 | convolution fusion | flops 828899328 | bytes 66191360 | tf_op jit(solution)/shard_map/dot_general | solution.py:56
  160.4 25.7 %all-gather.9.cloned.1.call-done = bf16[1,24,4,32,256]{4,3,1,2,0:T(8,128)(2,1)} async-done(((bf16[1,6,4,32,256]{4,3,1,2,0:T(8,128)(2,1)}), bf16[1,24,4,32,256]{4,3,1,2,0:T(8,128)(2,1)}) %all-gather.9.cloned.1.call-update) | async-done | bytes 1572880 | tf_op jit(solution)/shard_map/all_gather | solution.py:28
  214.9 7.1 %slice_bitcast_fusion.3 = (bf16[6,32,32,256]{3,1,0,2:T(8,128)(2,1)}, bf16[6,32,32,256]{3,1,0,2:T(8,128)(2,1)}, bf16[6,32,32,256]{3,1,0,2:T(8,128)(2,1)}) fusion(bf16[1,6,33,34,256]{4,2,1,3,0:T(8,128)(2,1)S(1)} %get-tuple-element.33), kind=kLoop, calls=%fused_computation.54 | loop fusion | bytes 18874368 | tf_op jit(solution)/shard_map/dot_general | solution.py:56
  229.3 21.6 %fusion.1 = (bf16[1,6,32,32,256]{4,2,1,3,0:T(8,128)(2,1)S(1)}, bf16[1,6,32,32,256]{4,2,1,3,0:T(8,128)(2,1)}) fusion(bf16[1,6,32,32,256]{4,3,2,1,0:T(8,128)(2,1)} %param.6, bf16[1,6,32,32,256]{4,2,1,3,0:T(8,128)(2,1)} %copy-done.2, bf16[3,3,256,256]{3,2,1,0:T(8,128)(2,1)} %get-tuple-element.47, bf16[1,6,33,34,256]{4,2,1,3,0:T(8,128)(2,1)S(1)} %get-tuple-element.33, ...), kind=kOutput, calls=%fused_computation.7 | convolution fusion | flops 839909376 | bytes 66191360 | tf_op jit(solution)/shard_map/dot_general | solution.py:56
  267.7 4.7 fusion.25
  277.0 4.7 fusion.19
  300.1 27.1 %fusion.164 = (bf16[1,6,34,34,256]{4,2,1,3,0:T(8,128)(2,1)}, f32[1,6,34,34,256]{4,2,1,3,0:T(8,128)}) fusion(bf16[3,3,256,256]{3,2,1,0:T(8,128)(2,1)} %get-tuple-element.47, bf16[1,6,32,32,256]{4,2,1,3,0:T(8,128)(2,1)S(1)} %get-tuple-element.12, f32[6,34,34,256]{3,1,0,2:T(8,128)} %fusion.28, f32[6,34,34,256]{3,1,0,2:T(8,128)} %fusion.25, ...), kind=kOutput, calls=%fused_computation.247 | convolution fusion | flops 925095936 | bytes 80777216 | tf_op jit(solution)/shard_map/dot_general | solution.py:93
  340.1 6.4 %convert_add_fusion = f32[1,6,32,32,256]{4,2,1,3,0:T(8,128)S(1)} fusion(f32[1,6,34,34,256]{4,2,1,3,0:T(8,128)} %get-tuple-element.65, bf16[1,6,32,32,256]{4,3,2,1,0:T(8,128)(2,1)} %param.6), kind=kLoop, calls=%fused_computation.4 | loop fusion | flops 3145728 | bytes 15728640 | tf_op jit(solution)/shard_map/add | solution.py:161
  357.7 13.4 %all-gather.11.cloned.1.call-done = bf16[1,24,4,32,256]{4,3,1,2,0:T(8,128)(2,1)} async-done(((bf16[1,6,4,32,256]{4,3,1,2,0:T(8,128)(2,1)}), bf16[1,24,4,32,256]{4,3,1,2,0:T(8,128)(2,1)}) %all-gather.11.cloned.1.call-update) | async-done | bytes 1572880 | tf_op jit(solution)/shard_map/all_gather | solution.py:33
  405.5 5.4 %reduce-scatter.5.cloned.1.call-done = f32[3,3,32,256]{3,2,1,0:T(8,128)} async-done(((f32[3,3,256,256]{3,2,1,0:T(8,128)}), f32[3,3,32,256]{3,2,1,0:T(8,128)}) %reduce-scatter.5.cloned.1.call-update) | async-done | bytes 294928 | tf_op jit(solution)/shard_map/reduce_scatter | solution.py:137
  410.8 38.1 %reduce-scatter.3.cloned.1.call-done = f32[3,3,32,256]{3,2,1,0:T(8,128)} async-done(((f32[3,3,256,256]{3,2,1,0:T(8,128)}), f32[3,3,32,256]{3,2,1,0:T(8,128)}) %reduce-scatter.3.cloned.1.call-update) | async-done | bytes 294928 | tf_op jit(solution)/shard_map/reduce_scatter | solution.py:137
  452.5 44.4 %all-reduce.4.cloned.1.call-done = (f32[3,3,32,256]{3,2,1,0:T(8,128)}, f32[3,3,32,256]{3,2,1,0:T(8,128)}) async-done(((f32[3,3,32,256]{3,2,1,0:T(8,128)}, f32[3,3,32,256]{3,2,1,0:T(8,128)}), (f32[3,3,32,256]{3,2,1,0:T(8,128)}, f32[3,3,32,256]{3,2,1,0:T(8,128)})) %all-reduce.4.cloned.1.call-update) | async-done | bytes 589840 | tf_op jit(solution)/shard_map/psum | solution.py:136
  (199 shorter events, 166.3 us)
Async XLA Ops:
  7.2 5.6 %copy-start.40 = (s32[6,4,3]{0,1,2:T(4,128)S(1)}, s32[6,4,3]{0,1,2:T(4,128)}, u32[]{:S(2)}) copy-start(s32[6,4,3]{0,1,2:T(4,128)} %param.7) | copy-start | bytes 868
  7.2 38.5 %all-gather.5.cloned.1.call-start = ((), (), s32[]{:S(2)}) async-start(), calls=%async_computation.2 | async-start | bytes 1966080 | tf_op jit(solution)/shard_map/all_gather | solution.py:28
  11.9 66.8 %all-gather.7.cloned.1.call-start = ((), (), s32[]{:S(2)}) async-start(), calls=%async_computation.3 | async-start | bytes 2654208 | tf_op jit(solution)/shard_map/all_gather | solution.py:141
  12.7 173.4 %all-gather.9.cloned.1.call-start = ((), (), s32[]{:S(2)}) async-start(), calls=%async_computation.4 | async-start | bytes 1966080 | tf_op jit(solution)/shard_map/all_gather | solution.py:28
  81.7 6.2 %copy-start.17 = (bf16[6,32,32,256]{3,2,1,0:T(8,128)(2,1)S(1)}, bf16[6,32,32,256]{3,2,1,0:T(8,128)(2,1)}, u32[]{:S(2)}) copy-start(bf16[6,32,32,256]{3,2,1,0:T(8,128)(2,1)} %get-tuple-element.29) | copy-start | bytes 9437188
  88.0 6.2 %copy-start.16 = (bf16[6,32,32,256]{3,2,1,0:T(8,128)(2,1)S(1)}, bf16[6,32,32,256]{3,2,1,0:T(8,128)(2,1)}, u32[]{:S(2)}) copy-start(bf16[6,32,32,256]{3,2,1,0:T(8,128)(2,1)} %get-tuple-element.27) | copy-start | bytes 9437188
  94.2 6.3 %copy-start.21 = (bf16[6,32,32,256]{3,2,1,0:T(8,128)(2,1)S(1)}, bf16[6,32,32,256]{3,2,1,0:T(8,128)(2,1)}, u32[]{:S(2)}) copy-start(bf16[6,32,32,256]{3,2,1,0:T(8,128)(2,1)} %get-tuple-element.41) | copy-start | bytes 9437188
  106.9 6.3 %copy-start.19 = (bf16[6,32,32,256]{3,2,1,0:T(8,128)(2,1)S(1)}, bf16[6,32,32,256]{3,2,1,0:T(8,128)(2,1)}, u32[]{:S(2)}) copy-start(bf16[6,32,32,256]{3,2,1,0:T(8,128)(2,1)} %get-tuple-element.40) | copy-start | bytes 9437188
  113.1 6.3 %copy-start.15 = (bf16[6,32,32,256]{3,2,1,0:T(8,128)(2,1)S(1)}, bf16[6,32,32,256]{3,2,1,0:T(8,128)(2,1)}, u32[]{:S(2)}) copy-start(bf16[6,32,32,256]{3,2,1,0:T(8,128)(2,1)} %get-tuple-element.67) | copy-start | bytes 9437188
  119.4 6.7 %copy-start.14 = (bf16[6,32,32,256]{3,2,1,0:T(8,128)(2,1)S(1)}, bf16[6,32,32,256]{3,2,1,0:T(8,128)(2,1)}, u32[]{:S(2)}) copy-start(bf16[6,32,32,256]{3,2,1,0:T(8,128)(2,1)} %get-tuple-element.66) | copy-start | bytes 9437188
  126.1 6.2 %copy-start.5 = (bf16[1,6,32,32,256]{4,3,2,1,0:T(8,128)(2,1)S(1)}, bf16[1,6,32,32,256]{4,3,2,1,0:T(8,128)(2,1)}, u32[]{:S(2)}) copy-start(bf16[1,6,32,32,256]{4,3,2,1,0:T(8,128)(2,1)} %param.4) | copy-start | bytes 9437188
  126.1 6.2 %copy-start.12 = (bf16[6,32,32,256]{3,2,1,0:T(8,128)(2,1)S(1)}, bf16[6,32,32,256]{3,2,1,0:T(8,128)(2,1)}, u32[]{:S(2)}) copy-start(bf16[6,32,32,256]{3,2,1,0:T(8,128)(2,1)} %get-tuple-element.68) | copy-start | bytes 9437188
  154.4 48.6 %copy-start.2 = (bf16[1,6,32,32,256]{4,2,1,3,0:T(8,128)(2,1)}, bf16[1,6,32,32,256]{4,2,1,3,0:T(8,128)(2,1)S(1)}, u32[]{:S(2)}) copy-start(bf16[1,6,32,32,256]{4,2,1,3,0:T(8,128)(2,1)S(1)} %get-tuple-element.62) | copy-start | bytes 9437188
  155.9 215.2 %all-gather.11.cloned.1.call-start = ((), (), s32[]{:S(2)}) async-start(), calls=%async_computation.5 | async-start | bytes 1966080 | tf_op jit(solution)/shard_map/all_gather | solution.py:33
  195.4 15.9 %copy-start = (bf16[1,6,33,34,256]{4,2,1,3,0:T(8,128)(2,1)}, bf16[1,6,33,34,256]{4,2,1,3,0:T(8,128)(2,1)S(1)}, u32[]{:S(2)}) copy-start(bf16[1,6,33,34,256]{4,2,1,3,0:T(8,128)(2,1)S(1)} %get-tuple-element.32) | copy-start | bytes 10340356
  203.5 18.5 %copy-start.25 = (bf16[6,32,32,256]{3,1,0,2:T(8,128)(2,1)}, bf16[6,32,32,256]{3,1,0,2:T(8,128)(2,1)S(1)}, u32[]{:S(2)}) copy-start(bf16[6,32,32,256]{3,1,0,2:T(8,128)(2,1)S(1)} %get-tuple-element.35) | copy-start | bytes 9437188
  203.5 22.1 %copy-start.23 = (bf16[6,32,32,256]{3,1,0,2:T(8,128)(2,1)}, bf16[6,32,32,256]{3,1,0,2:T(8,128)(2,1)S(1)}, u32[]{:S(2)}) copy-start(bf16[6,32,32,256]{3,1,0,2:T(8,128)(2,1)S(1)} %get-tuple-element.34) | copy-start | bytes 9437188
  340.1 70.8 %reduce-scatter.5.cloned.1.call-start = ((), (), s32[]{:S(2)}) async-start(), calls=%async_computation.7 | async-start | bytes 2654208 | tf_op jit(solution)/shard_map/reduce_scatter | solution.py:137
  346.6 4.6 copy-start.33
  346.6 4.6 copy-start.34
  357.6 19.9 %slice-start = ((s8[6291456]{0:T(1024)(128)(4,1)}), s8[2097152]{0:T(1024)(128)(4,1)S(1)}, s32[]{:S(2)}) async-start(s8[6291456]{0:T(1024)(128)(4,1)} %bitcast.433), calls=%async_computation.9 | async-start | bytes 4194304
  357.6 91.3 %reduce-scatter.3.cloned.1.call-start = ((), (), s32[]{:S(2)}) async-start(), calls=%async_computation.6 | async-start | bytes 2654208 | tf_op jit(solution)/shard_map/reduce_scatter | solution.py:137
  403.8 45.1 %copy-start.13 = (bf16[1,6,32,32,256]{4,2,1,3,0:T(8,128)(2,1)S(1)}, bf16[1,6,32,32,256]{4,2,1,3,0:T(8,128)(2,1)}, u32[]{:S(2)}) copy-start(bf16[1,6,32,32,256]{4,2,1,3,0:T(8,128)(2,1)} %get-tuple-element.13) | copy-start | bytes 9437188
  405.4 91.5 %all-reduce.4.cloned.1.call-start = ((), (), s32[]{:S(2)}) async-start(), calls=%async_computation.8 | async-start | bytes 1179648 | tf_op jit(solution)/shard_map/psum | solution.py:136
  (28 other events, 84.2 us)
Sparse Core Ops, SparseCore 0:
  12.0 33.5 all-gather.4
  47.2 31.4 all-gather.6
  156.0 30.0 all-gather.8
  340.2 30.8 all-gather.10
  373.8 36.9 reduce-scatter.4
  413.0 35.8 reduce-scatter.2
  451.9 44.9 all-reduce.3
where the time goes:
time: 513 us; the launch traced here: 506 us
  matrix products  228 us (44%)
  waiting for transfers between devices  163 us (32%)
  local copies, waits for them, and re-layouts  60.5 us (12%)
  other arithmetic  38.2 us (7%)
  between operations  15.1 us (3%)
    dot_general x18, matrix products, convolve(): jnp.dot(patches, kernel[row_off, col_off], preferred_element_type=jnp.flo...  125 us
    dot_general x9, matrix products, input_grad(): lax.dot_general(window, kernel[row_off, col_off], (((1,), (1,)), ((), ())...  64 us
    all_gather x2, waiting for transfers between devices, neighbor_rims(): lax.all_gather(edge_strips(tile_field), 'space', axis=1, tiled=True)  58.4 us
    psum x1, waiting for transfers between devices, reduce_grad(): space_total = lax.psum(partial_value, 'space')  44.4 us
    reduce_scatter x2, waiting for transfers between devices, reduce_grad(): return lax.psum_scatter(space_total, 'dp', scatter_dimension=2, tiled=True)  43.4 us
    dot_general x18, matrix products, weight_grad(): lax.dot_general(patches, flat_grad, (((0,), (0,)), ((), ())), preferred_e...  39.5 us
    dot_general x3, local copies, waits for them, and re-layouts, convolve(): jnp.dot(patches, kernel[row_off, col_off], preferred_element_type=jnp.flo...  21.7 us
    unnamed x97, local copies, waits for them, and re-layouts  15.4 us
  transfers between devices with their start and end apart: 7, of which 7 were waited for; matrix products, arithmetic and copies ran while one was open for 16% of the time, Pallas kernels for 0%

commit v1 on v0

--- a/solution.py
+++ b/solution.py
@@ -133,7 +133,7 @@
 
 
 def reduce_grad(partial_value):
-    space_total = lax.psum(partial_value, "space")
+    space_total = jnp.sum(lax.all_gather(partial_value, "space"), axis=0)
     return lax.psum_scatter(space_total, "dp", scatter_dimension=2, tiled=True)
 
 

time: 513 us -> 660 us (1.29)
  waiting for transfers between devices: 163 us -> 292 us
  other arithmetic: 38.2 us -> 49.8 us
    all_gather x0 -> x2, waiting for transfers between devices: none -> 153 us  [reduce_grad(): space_total = jnp.sum(lax.all_gather(partial_value, 'space'), axis=0)]
    psum x1 -> x0, waiting for transfers between devices: 44.4 us -> none  [reduce_grad(): space_total = lax.psum(partial_value, 'space')]
    reduce_scatter x2, waiting for transfers between devices: 43.4 us -> 67.8 us  [reduce_grad(): return lax.psum_scatter(space_total, 'dp', scatter_dimension=2, tiled=True)]
    reduce_sum x0 -> x2, other arithmetic: none -> 12.3 us  [reduce_grad(): space_total = jnp.sum(lax.all_gather(partial_value, 'space'), axis=0)]
    unnamed x97 -> x93, local copies, waits for them, and re-layouts: 15.4 us -> 20.4 us
  transfers between devices with their start and end apart: 7 -> 8, of which waited for: 7 -> 8; matrix products, arithmetic and copies ran while one was open for 16% -> 15% of each run, Pallas kernels for 0% -> 0%
where the time goes in v1:
time: 660 us; the launch traced here: 652 us
  waiting for transfers between devices  292 us (44%)
  matrix products  230 us (35%)
  local copies, waits for them, and re-layouts  64.9 us (10%)
  other arithmetic  49.8 us (8%)
  between operations  15.1 us (2%)
    all_gather x2, waiting for transfers between devices, reduce_grad(): space_total = jnp.sum(lax.all_gather(partial_value, 'space'), axis=0)  153 us
    dot_general x18, matrix products, convolve(): jnp.dot(patches, kernel[row_off, col_off], preferred_element_type=jnp.flo...  125 us
    reduce_scatter x2, waiting for transfers between devices, reduce_grad(): return lax.psum_scatter(space_total, 'dp', scatter_dimension=2, tiled=True)  67.8 us
    dot_general x9, matrix products, input_grad(): lax.dot_general(window, kernel[row_off, col_off], (((1,), (1,)), ((), ())...  63.9 us
    all_gather x2, waiting for transfers between devices, neighbor_rims(): lax.all_gather(edge_strips(tile_field), 'space', axis=1, tiled=True)  58.4 us
    dot_general x18, matrix products, weight_grad(): lax.dot_general(patches, flat_grad, (((0,), (0,)), ((), ())), preferred_e...  41.1 us
    dot_general x3, local copies, waits for them, and re-layouts, convolve(): jnp.dot(patches, kernel[row_off, col_off], preferred_element_type=jnp.flo...  21.8 us
    unnamed x93, local copies, waits for them, and re-layouts  20.4 us
  transfers between devices with their start and end apart: 8, of which 8 were waited for; matrix products, arithmetic and copies ran while one was open for 15% of the time, Pallas kernels for 0%

profile of v1, /device:TPU:0, one launch (start us, length us, event | category | flops | bytes accessed | tf_op | source)
XLA Modules:
  0.0 652.1 jit_solution(2437069379696422499)
XLA Ops:
  12.9 32.7 %all-gather.9.cloned.1.call-done = bf16[1,24,4,32,256]{4,3,1,2,0:T(8,128)(2,1)} async-done(((bf16[1,6,4,32,256]{4,3,1,2,0:T(8,128)(2,1)}), bf16[1,24,4,32,256]{4,3,1,2,0:T(8,128)(2,1)}) %all-gather.9.cloned.1.call-update) | async-done | bytes 1572880 | tf_op jit(solution)/shard_map/all_gather | solution.py:28
  51.8 5.4 fusion.38
  65.4 10.3 %slice_bitcast_fusion.9 = (bf16[6,32,32,256]{3,2,1,0:T(8,128)(2,1)}, bf16[6,32,32,256]{3,2,1,0:T(8,128)(2,1)}, bf16[6,32,32,256]{3,2,1,0:T(8,128)(2,1)}, bf16[6,...) fusion(bf16[1,6,33,34,256]{4,3,2,1,0:T(8,128)(2,1)S(1)} %get-tuple-element.31, ...), kind=kLoop, calls=%fused_computation.64 | loop fusion | bytes 37748736 | tf_op jit(solution)/shard_map/dot_general | solution.py:56
  81.7 6.2 fusion.39
  88.0 6.2 fusion.41
  94.2 6.3 fusion.43
  100.5 6.4 fusion.45
  106.9 6.3 fusion.47
  113.2 6.3 fusion.49
  119.5 6.8 %fusion.51 = f32[6,32,32,256]{3,1,0,2:T(8,128)} fusion(bf16[6,32,32,256]{3,2,1,0:T(8,128)(2,1)S(1)} %copy-done.17, bf16[3,3,256,256]{3,2,1,0:T(8,128)(2,1)S(1)} %get-tuple-element.46), kind=kOutput, calls=%fused_computation.84 | convolution fusion | flops 805306368 | bytes 9568256 | tf_op jit(solution)/shard_map/dot_general | solution.py:56
  126.2 6.2 fusion.53
  132.4 22.0 %fusion.5 = (bf16[1,6,32,32,256]{4,2,1,3,0:T(8,128)(2,1)S(1)}, f32[6,32,32,256]{3,1,0,2:T(8,128)}) fusion(bf16[1,6,32,32,256]{4,3,2,1,0:T(8,128)(2,1)S(1)} %copy-done.5, f32[6,32,32,256]{3,1,0,2:T(8,128)} %fusion.39, f32[6,32,32,256]{3,1,0,2:T(8,128)} %fusion.41, f32[6,32,32,256]{3,1,0,2:T(8,128)} %fusion.43, f32[6,32,32,256]{3,1,0,2:T(8,128)} %fusion.45, ...), kind=kOutput, calls=%fused_computation.15 | convolution fusion | flops 828899328 | bytes 66191360 | tf_op jit(solution)/shard_map/dot_general | solution.py:56
  160.5 25.7 %all-gather.13.cloned.1.call-done = bf16[1,24,4,32,256]{4,3,1,2,0:T(8,128)(2,1)} async-done(((bf16[1,6,4,32,256]{4,3,1,2,0:T(8,128)(2,1)}), bf16[1,24,4,32,256]{4,3,1,2,0:T(8,128)(2,1)}) %all-gather.13.cloned.1.call-update) | async-done | bytes 1572880 | tf_op jit(solution)/shard_map/all_gather | solution.py:28
  215.0 7.1 %slice_bitcast_fusion.3 = (bf16[6,32,32,256]{3,1,0,2:T(8,128)(2,1)}, bf16[6,32,32,256]{3,1,0,2:T(8,128)(2,1)}, bf16[6,32,32,256]{3,1,0,2:T(8,128)(2,1)}) fusion(bf16[1,6,33,34,256]{4,2,1,3,0:T(8,128)(2,1)S(1)} %get-tuple-element.33), kind=kLoop, calls=%fused_computation.54 | loop fusion | bytes 18874368 | tf_op jit(solution)/shard_map/dot_general | solution.py:56
  229.4 21.6 %fusion.1 = (bf16[1,6,32,32,256]{4,2,1,3,0:T(8,128)(2,1)S(1)}, bf16[1,6,32,32,256]{4,2,1,3,0:T(8,128)(2,1)}) fusion(bf16[1,6,32,32,256]{4,3,2,1,0:T(8,128)(2,1)} %param.6, bf16[1,6,32,32,256]{4,2,1,3,0:T(8,128)(2,1)} %copy-done.2, bf16[3,3,256,256]{3,2,1,0:T(8,128)(2,1)} %get-tuple-element.47, bf16[1,6,33,34,256]{4,2,1,3,0:T(8,128)(2,1)S(1)} %get-tuple-element.33, ...), kind=kOutput, calls=%fused_computation.7 | convolution fusion | flops 839909376 | bytes 66191360 | tf_op jit(solution)/shard_map/dot_general | solution.py:56
  300.1 27.1 %fusion.164 = (bf16[1,6,34,34,256]{4,2,1,3,0:T(8,128)(2,1)}, f32[1,6,34,34,256]{4,2,1,3,0:T(8,128)}) fusion(bf16[3,3,256,256]{3,2,1,0:T(8,128)(2,1)} %get-tuple-element.47, bf16[1,6,32,32,256]{4,2,1,3,0:T(8,128)(2,1)S(1)} %get-tuple-element.12, f32[6,34,34,256]{3,1,0,2:T(8,128)} %fusion.28, f32[6,34,34,256]{3,1,0,2:T(8,128)} %fusion.25, ...), kind=kOutput, calls=%fused_computation.247 | convolution fusion | flops 925095936 | bytes 80777216 | tf_op jit(solution)/shard_map/dot_general | solution.py:93
  349.1 5.5 convert_add_fusion
  360.7 8.5 %all-gather.15.cloned.1.call-done = bf16[1,24,4,32,256]{4,3,1,2,0:T(8,128)(2,1)} async-done(((bf16[1,6,4,32,256]{4,3,1,2,0:T(8,128)(2,1)}), bf16[1,24,4,32,256]{4,3,1,2,0:T(8,128)(2,1)}) %all-gather.15.cloned.1.call-update) | async-done | bytes 1572880 | tf_op jit(solution)/shard_map/all_gather | solution.py:33
  406.0 61.7 %all-gather.19.cloned.1.call-done = f32[12,3,256,256]{3,2,1,0:T(8,128)} async-done(((f32[3,3,256,256]{3,2,1,0:T(8,128)}), f32[12,3,256,256]{3,2,1,0:T(8,128)}) %all-gather.19.cloned.1.call-update) | async-done | bytes 9437200 | tf_op jit(solution)/shard_map/all_gather | solution.py:136
  467.7 6.1 reduce_sum.19
  474.1 91.6 %all-gather.17.cloned.1.call-done = f32[12,3,256,256]{3,2,1,0:T(8,128)} async-done(((f32[3,3,256,256]{3,2,1,0:T(8,128)}), f32[12,3,256,256]{3,2,1,0:T(8,128)}) %all-gather.17.cloned.1.call-update) | async-done | bytes 9437200 | tf_op jit(solution)/shard_map/all_gather | solution.py:136
  565.7 6.2 reduce_sum.18
  575.4 29.6 %reduce-scatter.5.cloned.1.call-done = f32[3,3,32,256]{3,2,1,0:T(8,128)} async-done(((f32[3,3,256,256]{3,2,1,0:T(8,128)}), f32[3,3,32,256]{3,2,1,0:T(8,128)}) %reduce-scatter.5.cloned.1.call-update) | async-done | bytes 294928 | tf_op jit(solution)/shard_map/reduce_scatter | solution.py:137
  605.0 38.2 %reduce-scatter.3.cloned.1.call-done = f32[3,3,32,256]{3,2,1,0:T(8,128)} async-done(((f32[3,3,256,256]{3,2,1,0:T(8,128)}), f32[3,3,32,256]{3,2,1,0:T(8,128)}) %reduce-scatter.3.cloned.1.call-update) | async-done | bytes 294928 | tf_op jit(solution)/shard_map/reduce_scatter | solution.py:137
  (199 shorter events, 187.0 us)
Async XLA Ops:
  7.2 5.6 copy-start.40
  7.2 38.5 %all-gather.9.cloned.1.call-start = ((), (), s32[]{:S(2)}) async-start(), calls=%async_computation.2 | async-start | bytes 1966080 | tf_op jit(solution)/shard_map/all_gather | solution.py:28
  11.9 66.8 %all-gather.11.cloned.1.call-start = ((), (), s32[]{:S(2)}) async-start(), calls=%async_computation.3 | async-start | bytes 2654208 | tf_op jit(solution)/shard_map/all_gather | solution.py:141
  12.7 173.5 %all-gather.13.cloned.1.call-start = ((), (), s32[]{:S(2)}) async-start(), calls=%async_computation.4 | async-start | bytes 1966080 | tf_op jit(solution)/shard_map/all_gather | solution.py:28
  81.7 6.2 copy-start.19
  88.0 6.2 copy-start.18
  94.2 6.3 copy-start.23
  106.9 6.3 copy-start.21
  113.2 6.3 copy-start.17
  119.5 6.8 %copy-start.16 = (bf16[6,32,32,256]{3,2,1,0:T(8,128)(2,1)S(1)}, bf16[6,32,32,256]{3,2,1,0:T(8,128)(2,1)}, u32[]{:S(2)}) copy-start(bf16[6,32,32,256]{3,2,1,0:T(8,128)(2,1)} %get-tuple-element.66) | copy-start | bytes 9437188
  126.2 6.2 copy-start.5
  126.2 6.2 copy-start.13
  154.4 48.6 %copy-start.2 = (bf16[1,6,32,32,256]{4,2,1,3,0:T(8,128)(2,1)}, bf16[1,6,32,32,256]{4,2,1,3,0:T(8,128)(2,1)S(1)}, u32[]{:S(2)}) copy-start(bf16[1,6,32,32,256]{4,2,1,3,0:T(8,128)(2,1)S(1)} %get-tuple-element.62) | copy-start | bytes 9437188
  155.9 213.3 %all-gather.15.cloned.1.call-start = ((), (), s32[]{:S(2)}) async-start(), calls=%async_computation.5 | async-start | bytes 1966080 | tf_op jit(solution)/shard_map/all_gather | solution.py:33
  195.4 15.9 %copy-start = (bf16[1,6,33,34,256]{4,2,1,3,0:T(8,128)(2,1)}, bf16[1,6,33,34,256]{4,2,1,3,0:T(8,128)(2,1)S(1)}, u32[]{:S(2)}) copy-start(bf16[1,6,33,34,256]{4,2,1,3,0:T(8,128)(2,1)S(1)} %get-tuple-element.32) | copy-start | bytes 10340356
  203.5 18.7 %copy-start.27 = (bf16[6,32,32,256]{3,1,0,2:T(8,128)(2,1)}, bf16[6,32,32,256]{3,1,0,2:T(8,128)(2,1)S(1)}, u32[]{:S(2)}) copy-start(bf16[6,32,32,256]{3,1,0,2:T(8,128)(2,1)S(1)} %get-tuple-element.35) | copy-start | bytes 9437188
  203.5 22.2 %copy-start.25 = (bf16[6,32,32,256]{3,1,0,2:T(8,128)(2,1)}, bf16[6,32,32,256]{3,1,0,2:T(8,128)(2,1)S(1)}, u32[]{:S(2)}) copy-start(bf16[6,32,32,256]{3,1,0,2:T(8,128)(2,1)S(1)} %get-tuple-element.34) | copy-start | bytes 9437188
  259.0 4.3 copy-start.29
  338.2 129.5 %all-gather.19.cloned.1.call-start = ((), (), s32[]{:S(2)}) async-start(), calls=%async_computation.9 | async-start | bytes 11796480 | tf_op jit(solution)/shard_map/all_gather | solution.py:136
  347.9 217.7 %all-gather.17.cloned.1.call-start = ((), (), s32[]{:S(2)}) async-start(), calls=%async_computation.8 | async-start | bytes 11796480 | tf_op jit(solution)/shard_map/all_gather | solution.py:136
  374.2 5.1 slice-start
  405.9 199.1 %reduce-scatter.5.cloned.1.call-start = ((), (), s32[]{:S(2)}) async-start(), calls=%async_computation.7 | async-start | bytes 2654208 | tf_op jit(solution)/shard_map/reduce_scatter | solution.py:137
  473.9 169.4 %reduce-scatter.3.cloned.1.call-start = ((), (), s32[]{:S(2)}) async-start(), calls=%async_computation.6 | async-start | bytes 2654208 | tf_op jit(solution)/shard_map/reduce_scatter | solution.py:137
  565.7 6.2 copy-start.14
  (27 other events, 74.7 us)
Sparse Core Ops, SparseCore 0:
  12.0 33.5 all-gather.8
  47.2 31.4 all-gather.10
  156.0 30.0 all-gather.12
  338.4 30.8 all-gather.14
  371.5 96.1 all-gather.18
  469.4 96.1 all-gather.16
  568.0 37.0 reduce-scatter.4
  607.3 35.8 reduce-scatter.2
